TPU v7x, 128 devices: a whole 4x4x4 slice. The times are simulated.
128 devices in a mesh: dp: 8 (over x, core), mp: 16 (over z, y).
Axes of the slice: x: 4, y: 4, z: 4, core: 2. Of those that a mesh axis runs over, the one named last changes fastest.
Arguments:
- canvas: bfloat16 [16, 16, 16, 1408], P('dp'), may hold values from -6 to 6
- target: bfloat16 [16, 16, 16, 1408], P('dp'), may hold values from -6 to 6
- kernel: float32 [49, 1408], replicated, may hold values from -0.875 to 0.875
- kernel_bias: float32 [1408], replicated, may hold values from -3 to 3
- norm_gain: float32 [1408], replicated, may hold values from 0.5 to 1.5
- norm_bias: float32 [1408], replicated, may hold values from -2 to 2
- in_weight: bfloat16 [5632, 1408], P('mp'), may hold values from -0.15625 to 0.15625
- in_bias: float32 [5632], P('mp'), may hold values from -3 to 3
- out_weight: bfloat16 [5632, 1408], P('mp'), may hold values from -0.078125 to 0.078125
- out_bias: float32 [1408], replicated, may hold values from -3 to 3
- probe_vector: float32 [49, 1408], P(None, 'mp'), may hold values from -6 to 6
- shapes: int32 [16, 2], P('dp'), may hold values from 2 to 16, as said below
- send_slots: int32 [16, 16, 16], P('dp'), may hold values from -1 to 447, as said below
Outputs:
- krylov_vector: float32 [49, 1408], P(None, 'mp')
- first_rayleigh: float32 [1], replicated
- lanczos_terms: float32 [3], replicated
Inputs may be any that keep to these rules, and one draw needn't show every extreme that they name: `shapes`: one of an image's two sides equals 16. `send_slots`: A cell's entry is -1 exactly where it lies outside its image; otherwise it is d * 56 + k: the cell goes to slot k of the owner with dp index d. No two cells of one dp index share an entry, so none sends more than 56 cells to one owner; every owner receives exactly 256 cells over all dp indices; some dp index sends 56 cells to every owner.
All inputs are finite; a program needn't handle non-finite values.
Results may differ from a plain program's by a relative error of at most 0.025.
Values may be sent and summed in bfloat16 or wider, within the bound.
A program may use at most 128 MiB of HBM per device.

v0:
```python
import jax
import jax.numpy as jnp
from jax import lax
from jax.sharding import PartitionSpec as P

C = 1408
KS = 7
SIDE = 16
MOST_SRC = 448
OWN = 256
layer_eps = 1e-06
vector_eps = 1e-06
half_root = 0.7071067811865476
density_scale = 0.3989422804014327


def phi_density(values):
    return density_scale * jnp.exp(-0.5 * values * values)


def gelu_value(values):
    return 0.5 * values * (1.0 + jax.scipy.special.erf(values * half_root))


def gelu_slope(values):
    return 0.5 * (1.0 + jax.scipy.special.erf(values * half_root)) + values * phi_density(values)


def gelu_bend(values):
    return phi_density(values) * (2.0 - values * values)


def inside_mask(shapes):
    cell_axis = jnp.arange(SIDE, dtype=jnp.int32)
    tall = cell_axis[None, :, None] < shapes[:, 0][:, None, None]
    wide = cell_axis[None, None, :] < shapes[:, 1][:, None, None]
    return (tall & wide).astype(jnp.float32)


def depthwise(canvas_values, tap_weights):
    margin_cells = KS // 2
    padded = jnp.pad(
        canvas_values, ((0, 0), (margin_cells, margin_cells), (margin_cells, margin_cells), (0, 0))
    )
    running = jnp.zeros(canvas_values.shape, jnp.float32)
    for tap_row in range(KS):
        for tap_col in range(KS):
            running = (
                running
                + padded[:, tap_row : tap_row + SIDE, tap_col : tap_col + SIDE, :]
                * tap_weights[tap_row * KS + tap_col]
            )
    return running


def correlate(masked, grads):
    margin_cells = KS // 2
    padded = jnp.pad(
        masked, ((0, 0), (margin_cells, margin_cells), (margin_cells, margin_cells), (0, 0))
    )
    pieces = []
    for tap_row in range(KS):
        for tap_col in range(KS):
            window = padded[:, tap_row : tap_row + SIDE, tap_col : tap_col + SIDE, :]
            pieces.append(
                jnp.einsum("npqc,npqc->c", window, grads, preferred_element_type=jnp.float32)
            )
    return jnp.stack(pieces, 0)


def normalize(rows):
    values = rows.astype(jnp.float32)
    row_mean = jnp.mean(values, 1, keepdims=True)
    centered = values - row_mean
    deviation = jnp.sqrt(jnp.mean(centered * centered, 1, keepdims=True) + layer_eps)
    return (centered / deviation, deviation)


def model_sum(partial_value):
    return lax.psum(partial_value.astype(jnp.bfloat16), "mp").astype(jnp.float32)


def input_share(partial_value):
    return lax.psum_scatter(
        partial_value.astype(jnp.bfloat16), "mp", scatter_dimension=1, tiled=True
    ).astype(jnp.float32)


def row_stats(first_sum, second_sum):
    return lax.psum((first_sum, second_sum), "mp")


def inner_model(first_vec, second_vec):
    return lax.psum(jnp.sum(first_vec * second_vec), "mp")


def alpha_of(product, direction):
    return inner_model(product, direction)


def per_device(
    canvas,
    target,
    kernel,
    kernel_bias,
    norm_gain,
    norm_bias,
    in_weight,
    in_bias,
    out_weight,
    out_bias,
    probe_vector,
    shapes,
    send_slots,
):
    sources = lax.axis_size("dp")
    models = lax.axis_size("mp")
    model_index = lax.axis_index("mp")
    images = canvas.shape[0]
    cell_count = images * SIDE * SIDE
    shard_width = C // models
    capacity = MOST_SRC // sources
    slot_count = sources * capacity
    tokens = OWN * sources
    channel_start = model_index * shard_width
    inside = inside_mask(shapes)
    masked = canvas * inside[..., None].astype(jnp.bfloat16)
    masked_part = lax.dynamic_slice_in_dim(masked, channel_start, shard_width, 3)
    flat_slots = send_slots.reshape(cell_count)
    slot_hits = flat_slots[None, :] == jnp.arange(slot_count, dtype=jnp.int32)[:, None]
    source_cell = jnp.sum(
        jnp.where(slot_hits, jnp.arange(cell_count, dtype=jnp.int32)[None, :], 0), axis=1
    )
    slot_flags = jnp.any(slot_hits, axis=1).astype(jnp.bfloat16).reshape(sources, capacity)

    def pack_slots(values):
        return jnp.take(values, source_cell, axis=0).reshape(sources, capacity, values.shape[1])

    conv_source = masked.astype(jnp.float32)
    conved = (depthwise(conv_source, kernel) + kernel_bias).astype(jnp.bfloat16)
    diff = (target.astype(jnp.float32) - canvas.astype(jnp.float32)).astype(jnp.bfloat16)
    payload = jnp.stack([conved.reshape(cell_count, C), diff.reshape(cell_count, C)], 1).reshape(
        cell_count, 2 * C
    )
    arrived_rows, arrived_flags = (
        lax.all_to_all(pack_slots(payload), "dp", split_axis=0, concat_axis=0, tiled=True),
        lax.all_to_all(slot_flags, "dp", split_axis=0, concat_axis=0, tiled=True),
    )
    gather_live_slots = arrived_flags.reshape(slot_count) > 0.5
    live_count = gather_live_slots.astype(jnp.int32)
    gather_position = jnp.cumsum(live_count) - live_count
    row_marks = gather_live_slots[None, :] & (
        gather_position[None, :] == jnp.arange(OWN, dtype=jnp.int32)[:, None]
    )
    gather_slot_of_row = jnp.sum(
        jnp.where(row_marks, jnp.arange(slot_count, dtype=jnp.int32)[None, :], 0), axis=1
    )
    owned_rows = jnp.take(
        arrived_rows.reshape(slot_count, 2 * C), gather_slot_of_row, axis=0
    ).reshape(OWN, 2, C)
    conv_rows = owned_rows[:, 0]
    diff_rows = owned_rows[:, 1]
    normed, deviation = normalize(conv_rows)
    features = (normed * norm_gain + norm_bias).astype(jnp.bfloat16)
    pre_act = (
        jnp.einsum("tc,hc->th", features, in_weight, preferred_element_type=jnp.float32) + in_bias
    )
    activation = gelu_value(pre_act).astype(jnp.bfloat16)
    outputs = (
        model_sum(jnp.dot(activation, out_weight, preferred_element_type=jnp.float32)) + out_bias
    )
    residue = (outputs - diff_rows.astype(jnp.float32)).astype(jnp.bfloat16)
    back_act = jnp.einsum("tc,hc->th", residue, out_weight, preferred_element_type=jnp.float32)
    slope = gelu_slope(pre_act)
    curvature = back_act * gelu_bend(pre_act)
    back_pre = (back_act * slope).astype(jnp.bfloat16)
    back_feat = input_share(jnp.dot(back_pre, in_weight, preferred_element_type=jnp.float32))
    gain_part = lax.dynamic_slice_in_dim(norm_gain, channel_start, shard_width, 0)
    normed_part = lax.dynamic_slice_in_dim(normed, channel_start, shard_width, 1)
    grad_scaled = back_feat * gain_part
    grad_total, grad_cross = row_stats(
        jnp.sum(grad_scaled, 1), jnp.sum(grad_scaled * normed_part, 1)
    )
    grad_mean = grad_total[:, None] / C
    grad_corr = grad_cross[:, None] / C
    back_conv = (grad_scaled - grad_mean - normed_part * grad_corr) / deviation
    safe_slots = jnp.maximum(flat_slots, 0)

    def hessian(direction):
        full_direction = lax.all_gather(direction, "mp", axis=1, tiled=True)
        tangent = depthwise(conv_source, full_direction).astype(jnp.bfloat16).reshape(cell_count, C)
        arrived_tan = lax.all_to_all(
            pack_slots(tangent), "dp", split_axis=0, concat_axis=0, tiled=True
        )
        tan_rows = jnp.take(arrived_tan.reshape(slot_count, C), gather_slot_of_row, axis=0)
        tangent_vals = tan_rows.astype(jnp.float32)
        lift = jnp.mean(normed * tangent_vals, 1, keepdims=True)
        tan_hat = (
            tangent_vals - jnp.mean(tangent_vals, 1, keepdims=True) - normed * lift
        ) / deviation
        rate = lift / deviation
        tan_feat = (tan_hat * norm_gain).astype(jnp.bfloat16)
        tan_pre = jnp.einsum("tc,hc->th", tan_feat, in_weight, preferred_element_type=jnp.float32)
        tan_act = (slope * tan_pre).astype(jnp.bfloat16)
        tan_out = model_sum(
            jnp.dot(tan_act, out_weight, preferred_element_type=jnp.float32)
        ).astype(jnp.bfloat16)
        tan_back_act = jnp.einsum(
            "tc,hc->th", tan_out, out_weight, preferred_element_type=jnp.float32
        )
        tan_back_pre = (tan_back_act * slope + curvature * tan_pre).astype(jnp.bfloat16)
        tan_scaled = (
            input_share(jnp.dot(tan_back_pre, in_weight, preferred_element_type=jnp.float32))
            * gain_part
        )
        tan_hat_part = lax.dynamic_slice_in_dim(tan_hat, channel_start, shard_width, 1)
        tan_total, tan_cross = row_stats(
            jnp.sum(tan_scaled, 1),
            jnp.sum(tan_scaled * normed_part + grad_scaled * tan_hat_part, 1),
        )
        tan_mean = tan_total[:, None] / C
        tan_corr = tan_cross[:, None] / C
        tan_back = (
            (tan_scaled - tan_mean - tan_hat_part * grad_corr - normed_part * tan_corr) / deviation
            - back_conv * rate
        ).astype(jnp.bfloat16)
        at_slots = jnp.take(tan_back, gather_position, axis=0)
        at_slots = jnp.where(gather_live_slots[:, None], at_slots, jnp.zeros_like(at_slots))
        returned = lax.all_to_all(
            at_slots.reshape(sources, capacity, shard_width),
            "dp",
            split_axis=0,
            concat_axis=0,
            tiled=True,
        )
        cell_values = jnp.take(returned.reshape(slot_count, shard_width), safe_slots, axis=0)
        cell_values = jnp.where(flat_slots[:, None] >= 0, cell_values, jnp.zeros_like(cell_values))
        local_term = correlate(
            masked_part, cell_values.reshape(images, SIDE, SIDE, shard_width)
        ) * (1.0 / tokens)
        return (lax.psum(local_term, "dp"), local_term)

    probe_norm = jnp.sqrt(inner_model(probe_vector, probe_vector) + vector_eps)
    lanczos_one = probe_vector / probe_norm
    product_one, local_one = hessian(lanczos_one)
    alpha_one = alpha_of(product_one, lanczos_one)
    remainder_one = product_one - alpha_one * lanczos_one
    beta_one = jnp.sqrt(inner_model(remainder_one, remainder_one) + vector_eps)
    lanczos_two = remainder_one / beta_one
    product_two, local_two = hessian(lanczos_two)
    alpha_two = alpha_of(product_two, lanczos_two)
    remainder_two = product_two - alpha_two * lanczos_two - beta_one * lanczos_one
    beta_two = jnp.sqrt(inner_model(remainder_two, remainder_two) + vector_eps)
    return (
        remainder_two / beta_two,
        jnp.stack([alpha_one]),
        jnp.stack([alpha_two, beta_one, beta_two]),
    )


def solution(mesh):
    placed = (
        P("dp", None, None, None),
        P("dp", None, None, None),
        P(),
        P(),
        P(),
        P(),
        P("mp", None),
        P("mp"),
        P("mp", None),
        P(),
        P(None, "mp"),
        P("dp", None),
        P("dp", None, None),
    )
    return jax.shard_map(
        per_device, mesh=mesh, in_specs=placed, out_specs=(P(None, "mp"), P(), P()), check_vma=False
    )
```

profile of v0, /device:TPU:0, one launch (start us, length us, event | category | flops | bytes accessed | tf_op | source)
XLA Modules:
  0.0 1089.0 jit_solution(18031086385054804951)
XLA Ops:
  9.0 4.4 all-to-all-start
  20.0 42.6 %psum.112 = f32[]{:T(128)} all-reduce(f32[]{:T(128)} %multiply_reduce_fusion.5), channel_id=1, replica_groups=mesh['dp'=8,'mp'=16] {'mp'}, use_global_device_ids=true, to_apply=%region_8.9 | all-reduce | flops 1 | bytes 8 | tf_op jit(solution)/shard_map/psum | solution.py:94
  64.0 21.0 %all-gather = f32[16,88,49]{1,2,0:T(8,128)S(1)} all-gather(f32[1,88,49]{1,2,0:T(8,128)S(1)} %fusion.195), channel_id=1, replica_groups=mesh['dp'=8,'mp'=16] {'mp'}, dimensions={0}, use_global_device_ids=true | all-gather | bytes 293216 | tf_op jit(solution)/shard_map/all_gather | solution.py:190
  87.9 19.6 %add_convert_fusion.2 = bf16[2,16,16,1408]{3,2,1,0:T(8,128)(2,1)S(1)} fusion(bf16[2,16,16,1408]{3,2,1,0:T(8,128)(2,1)S(1)} %get-tuple-element.279, f32[2,16,16,1408]{3,2,1,0:T(8,128)S(1)} %get-tuple-element.278, f32[1408]{0:T(1024)S(1)} %copy-done.48, f32[1408]{0:T(1024)S(1)} %get-tuple-element.109, f32[1408]{0:T(1024)S(1)} %get-tuple-element.110, ...), kind=kLoop, calls=%fused_computation.160 | loop fusion | flops 72089600 | bytes 6048768 | tf_op jit(solution)/shard_map/convert_element_type | solution.py:140
  112.5 8.1 pad_maximum_fusion
  120.6 19.7 %add_convert_fusion.1 = bf16[2,16,16,1408]{3,2,1,0:T(8,128)(2,1)S(1)} fusion(bf16[2,16,16,1408]{3,2,1,0:T(8,128)(2,1)S(1)} %get-tuple-element.279, f32[2,16,16,1408]{3,2,1,0:T(8,128)S(1)} %get-tuple-element.278, f32[1408]{0:T(1024)S(1)} %get-tuple-element.112, f32[1408]{0:T(1024)S(1)} %get-tuple-element.113, f32[1408]{0:T(1024)S(1)} %get-tuple-element.114, ...), kind=kLoop, calls=%fused_computation.158 | loop fusion | flops 71368704 | bytes 6043136 | tf_op jit(solution)/shard_map/convert_element_type | solution.py:191
  145.9 3.8 copy.746
  149.7 4.8 all-to-all-start.2
  154.6 8.7 gather_fusion
  166.7 6.0 all-to-all-done.2
  180.4 4.2 gather_fusion.3
  184.6 24.6 %all-to-all-done.1 = bf16[8,56,2816]{2,1,0:T(8,128)(2,1)S(1)} async-done(((bf16[8,56,2816]{2,1,0:T(8,128)(2,1)}), bf16[8,56,2816]{2,1,0:T(8,128)(2,1)S(1)}, u32[]{:S(2)}, u32[]{:S(2)}) %all-to-all-start.1) | async-done | bytes 2523168 | tf_op jit(solution)/shard_map/all_to_all | solution.py:146
  224.8 86.0 %all-reduce.14.cloned.1.call-done = (bf16[256,1408]{1,0:T(8,128)(2,1)}, bf16[256,1408]{1,0:T(8,128)(2,1)}) async-done(((bf16[256,1408]{1,0:T(8,128)(2,1)}, bf16[256,1408]{1,0:T(8,128)(2,1)}), (bf16[256,1408]{1,0:T(8,128)(2,1)}, bf16[256,1408]{1,0:T(8,128)(2,1)})) %all-reduce.14.cloned.1.call-update) | async-done | bytes 1441808 | tf_op jit(solution)/shard_map/psum | solution.py:80
  319.9 67.5 %reduce-scatter.12.cloned.1.call-done = bf16[256,88]{0,1:T(8,128)(2,1)} async-done(((bf16[256,1408]{0,1:T(8,128)(2,1)}), bf16[256,88]{0,1:T(8,128)(2,1)}) %reduce-scatter.12.cloned.1.call-update) | async-done | bytes 45072
  388.4 74.6 %reduce-scatter.10.cloned.1.call-done = bf16[256,88]{0,1:T(8,128)(2,1)} async-done(((bf16[256,1408]{0,1:T(8,128)(2,1)}), bf16[256,88]{0,1:T(8,128)(2,1)}) %reduce-scatter.10.cloned.1.call-update) | async-done | bytes 45072
  465.3 38.1 %all-reduce.7 = (f32[256]{0:T(256)S(1)}, f32[256]{0:T(256)S(1)}, f32[256]{0:T(256)S(1)}, f32[256]{0:T(256)S(1)}) all-reduce(f32[256]{0:T(256)S(1)} %get-tuple-element.261, f32[256]{0:T(256)S(1)} %get-tuple-element.8, f32[256]{0:T(256)S(1)} %get-tuple-element.6, f32[256]{0:T(256)S(1)} %get-tuple-element.258), channel_id=1, replica_groups=mesh['dp'=8,'mp'=16] {'mp'}, use_global_device_ids=true, to_apply=%region_22.25 | all-reduce | flops 1024 | bytes 8192 | tf_op jit(solution)/shard_map/psum | solution.py:90
  507.6 4.3 all-to-all-start.3
  512.0 5.9 all-to-all-done.3
  521.4 23.9 %psum.119 = f32[49,88]{1,0:T(8,128)S(1)} all-reduce(f32[49,88]{1,0:T(8,128)S(1)} %broadcast_multiply_fusion.2), channel_id=1, replica_groups=mesh['dp'=8,'mp'=16] {'dp'}, use_global_device_ids=true, to_apply=%region_23.28 | all-reduce | flops 4312 | bytes 34496 | tf_op jit(solution)/shard_map/psum | solution.py:241
  545.8 36.1 %psum.120 = f32[]{:T(128)} all-reduce(f32[]{:T(128)} %multiply_reduce_fusion.4), channel_id=1, replica_groups=mesh['dp'=8,'mp'=16] {'mp'}, use_global_device_ids=true, to_apply=%region_25.30 | all-reduce | flops 1 | bytes 8 | tf_op jit(solution)/shard_map/psum | solution.py:94
  583.2 38.1 %psum.121 = f32[]{:T(128)} all-reduce(f32[]{:T(128)} %multiply_reduce_fusion.3), channel_id=1, replica_groups=mesh['dp'=8,'mp'=16] {'mp'}, use_global_device_ids=true, to_apply=%region_27.32 | all-reduce | flops 1 | bytes 8 | tf_op jit(solution)/shard_map/psum | solution.py:94
  622.6 21.2 %all-gather.1 = f32[16,88,49]{1,2,0:T(8,128)S(1)} all-gather(f32[1,88,49]{1,2,0:T(8,128)S(1)} %fusion.194), channel_id=1, replica_groups=mesh['dp'=8,'mp'=16] {'mp'}, dimensions={0}, use_global_device_ids=true | all-gather | bytes 293216 | tf_op jit(solution)/shard_map/all_gather | solution.py:190
  644.9 80.7 %add_convert_fusion = bf16[2,16,16,1408]{3,2,1,0:T(8,128)(2,1)S(1)} fusion(bf16[2,16,16,1408]{3,2,1,0:T(8,128)(2,1)} %copy-done.3, f32[2,16,16,1408]{3,2,1,0:T(8,128)} %copy-done.1, f32[1408]{0:T(1024)S(1)} %get-tuple-element.14, f32[1408]{0:T(1024)S(1)} %get-tuple-element.15, f32[1408]{0:T(1024)S(1)} %get-tuple-element.16, f32[1408]{0:T(1024)S(1)} %get-tuple-element.17, ...), kind=kLoop, calls=%fused_computation.157 | loop fusion | flops 71368704 | bytes 6043136 | tf_op jit(solution)/shard_map/convert_element_type | solution.py:191
  730.1 20.7 %all_to_all.31 = bf16[8,56,1408]{2,1,0:T(8,128)(2,1)S(1)} all-to-all(bf16[8,56,1408]{2,1,0:T(8,128)(2,1)S(1)} %bitcast.832), channel_id=1, replica_groups=mesh['dp'=8,'mp'=16] {'dp'}, dimensions={0} | all-to-all | bytes 2523136 | tf_op jit(solution)/shard_map/all_to_all | solution.py:192
  760.3 83.7 %all-reduce.12.cloned.1.call-done = bf16[256,1408]{1,0:T(8,128)(2,1)} async-done(((bf16[256,1408]{1,0:T(8,128)(2,1)}), bf16[256,1408]{1,0:T(8,128)(2,1)}) %all-reduce.12.cloned.1.call-update) | async-done | bytes 720912 | tf_op jit(solution)/shard_map/psum | solution.py:80
  844.0 3.9 convolution_convert_fusion
  848.0 72.4 %reduce-scatter.14.cloned.1.call-done = bf16[256,88]{0,1:T(8,128)(2,1)} async-done(((bf16[256,1408]{0,1:T(8,128)(2,1)}), bf16[256,88]{0,1:T(8,128)(2,1)}) %reduce-scatter.14.cloned.1.call-update) | async-done | bytes 45072
  922.6 38.1 %all-reduce.6 = (f32[256]{0:T(256)S(1)}, f32[256]{0:T(256)S(1)}) all-reduce(f32[256]{0:T(256)S(1)} %get-tuple-element.260, f32[256]{0:T(256)S(1)} %get-tuple-element.259), channel_id=1, replica_groups=mesh['dp'=8,'mp'=16] {'mp'}, use_global_device_ids=true, to_apply=%region_35.40 | all-reduce | flops 512 | bytes 4096 | tf_op jit(solution)/shard_map/psum | solution.py:90
  964.6 10.2 all_to_all.32
  978.3 23.9 %psum.125 = f32[49,88]{1,0:T(8,128)S(1)} all-reduce(f32[49,88]{1,0:T(8,128)S(1)} %broadcast_multiply_fusion.1), channel_id=1, replica_groups=mesh['dp'=8,'mp'=16] {'dp'}, use_global_device_ids=true, to_apply=%region_36.41 | all-reduce | flops 4312 | bytes 34496 | tf_op jit(solution)/shard_map/psum | solution.py:241
  1003.5 36.2 %psum.126 = f32[]{:T(128)} all-reduce(f32[]{:T(128)} %multiply_reduce_fusion.2), channel_id=1, replica_groups=mesh['dp'=8,'mp'=16] {'mp'}, use_global_device_ids=true, to_apply=%region_38.43 | all-reduce | flops 1 | bytes 8 | tf_op jit(solution)/shard_map/psum | solution.py:94
  1041.6 38.1 %psum.127 = f32[]{:T(128)} all-reduce(f32[]{:T(128)} %get-tuple-element.272), channel_id=1, replica_groups=mesh['dp'=8,'mp'=16] {'mp'}, use_global_device_ids=true, to_apply=%region_40.45 | all-reduce | flops 1 | bytes 8 | tf_op jit(solution)/shard_map/psum | solution.py:94
  (256 shorter events, 101.0 us)
Async XLA Ops:
  7.2 214.5 %copy-start = (bf16[352,1408]{1,0:T(8,128)(2,1)S(1)}, bf16[352,1408]{1,0:T(8,128)(2,1)}, u32[]{:S(2)}) copy-start(bf16[352,1408]{1,0:T(8,128)(2,1)} %param.29) | copy-start | bytes 2973700
  7.2 80.1 %copy-start.13 = (bf16[2,16,16,1408]{3,2,1,0:T(8,128)(2,1)S(1)}, bf16[2,16,16,1408]{3,2,1,0:T(8,128)(2,1)}, u32[]{:S(2)}) copy-start(bf16[2,16,16,1408]{3,2,1,0:T(8,128)(2,1)} %param.21) | copy-start | bytes 4325380
  9.0 140.7 %all-to-all-start = ((bf16[8,1,56]{2,1,0:T(2,128)(2,1)}), bf16[8,1,56]{2,1,0:T(2,128)(2,1)}, u32[]{:S(2)}, u32[]{:S(2)}) async-start(bf16[8,1,56]{2,1,0:T(2,128)(2,1)} %reshape.856), calls=%async_computation | async-start | bytes 8192 | tf_op jit(solution)/shard_map/all_to_all | solution.py:147
  86.1 57.1 %copy-start.55 = (pred[448]{0:T(512)(128)(4,1)}, pred[448]{0:T(512)(128)(4,1)S(1)}, u32[]{:S(2)}) copy-start(pred[448]{0:T(512)(128)(4,1)S(1)} %compare_and_fusion.2) | copy-start | bytes 1348
  149.7 23.1 %all-to-all-start.2 = ((bf16[8,56,1408]{2,1,0:T(8,128)(2,1)}), bf16[8,56,1408]{2,1,0:T(8,128)(2,1)S(1)}, u32[]{:S(2)}, u32[]{:S(2)}) async-start(bf16[8,56,1408]{2,1,0:T(8,128)(2,1)} %bitcast.212), calls=%async_computation.2 | async-start | bytes 2523136 | tf_op jit(solution)/shard_map/all_to_all | solution.py:192
  173.9 35.3 %all-to-all-start.1 = ((bf16[8,56,2816]{2,1,0:T(8,128)(2,1)}), bf16[8,56,2816]{2,1,0:T(8,128)(2,1)S(1)}, u32[]{:S(2)}, u32[]{:S(2)}) async-start(bf16[8,56,2816]{2,1,0:T(8,128)(2,1)} %broadcast_select_fusion), calls=%async_computation.1 | async-start | bytes 5046272 | tf_op jit(solution)/shard_map/all_to_all | solution.py:146
  177.5 133.3 %all-reduce.14.cloned.1.call-start = ((), (), s32[]{:S(2)}) async-start(), calls=%async_computation.13 | async-start | bytes 2883584 | tf_op jit(solution)/shard_map/psum | solution.py:80
  217.1 93.7 %copy-start.4 = (bf16[256,2,1408]{2,0,1:T(8,128)(2,1)}, bf16[256,2,1408]{2,0,1:T(8,128)(2,1)S(1)}, u32[]{:S(2)}) copy-start(bf16[256,2,1408]{2,0,1:T(8,128)(2,1)S(1)} %broadcast_select_fusion.1) | copy-start | bytes 4325380
  221.7 89.1 %copy-start.58 = (f32[1408]{0:T(1024)S(1)}, f32[1408]{0:T(1024)}, u32[]{:S(2)}) copy-start(f32[1408]{0:T(1024)} %param.30) | copy-start | bytes 16900
  224.7 162.7 %reduce-scatter.12.cloned.1.call-start = ((), (), s32[]{:S(2)}) async-start(), calls=%async_computation.11 | async-start | bytes 765952
  314.9 148.1 %reduce-scatter.10.cloned.1.call-start = ((), (), s32[]{:S(2)}) async-start(), calls=%async_computation.10 | async-start | bytes 765952
  314.9 188.9 %copy-start.27 = (f32[256]{0:T(256)S(1)}, f32[256]{0:T(256)}, u32[]{:S(2)}) copy-start(f32[256]{0:T(256)} %copy-done.26) | copy-start | bytes 3076
  314.9 188.9 %copy-start.56 = (f32[256]{0:T(256)S(1)}, f32[256]{0:T(256)}, u32[]{:S(2)}) copy-start(f32[256]{0:T(256)} %get-tuple-element.285) | copy-start | bytes 3076
  315.0 191.8 %copy-start.44 = (pred[448]{0:T(512)(128)(4,1)S(1)}, pred[448]{0:T(512)(128)(4,1)}, u32[]{:S(2)}) copy-start(pred[448]{0:T(512)(128)(4,1)} %copy-done.43) | copy-start | bytes 1348
  315.0 191.8 %copy-start.50 = (pred[448]{0:T(512)(128)(4,1)S(1)}, pred[448]{0:T(512)(128)(4,1)}, u32[]{:S(2)}) copy-start(pred[448]{0:T(512)(128)(4,1)} %get-tuple-element.276) | copy-start | bytes 1348
  318.7 226.6 %copy-start.19 = (f32[49,88]{1,0:T(8,128)S(1)}, f32[49,88]{1,0:T(8,128)}, u32[]{:S(2)}) copy-start(f32[49,88]{1,0:T(8,128)} %param.31) | copy-start | bytes 51748
  318.8 184.6 %copy-start.49 = (f32[88]{0:T(128)}, f32[88]{0:T(128)S(1)}, u32[]{:S(2)}) copy-start(f32[88]{0:T(128)S(1)} %dynamic_slice.16) | copy-start | bytes 1060
  319.8 324.0 %copy-start.51 = (pred[512]{0:T(512)(128)(4,1)}, pred[512]{0:T(512)(128)(4,1)S(1)}, u32[]{:S(2)}) copy-start(pred[512]{0:T(512)(128)(4,1)S(1)} %get-tuple-element.281) | copy-start | bytes 1540
  319.9 324.0 %copy-start.53 = (pred[512]{0:T(512)(128)(4,1)}, pred[512]{0:T(512)(128)(4,1)S(1)}, u32[]{:S(2)}) copy-start(pred[512]{0:T(512)(128)(4,1)S(1)} %get-tuple-element.282) | copy-start | bytes 1540
  319.9 199.3 %copy-start.36 = (s32[1024]{0:T(1024)}, s32[1024]{0:T(1024)S(1)}, u32[]{:S(2)}) copy-start(s32[1024]{0:T(1024)S(1)} %pad_clamp_fusion.1) | copy-start | bytes 12292
  388.4 119.3 %copy-start.14 = (bf16[256,88]{1,0:T(8,128)(2,1)}, bf16[256,88]{1,0:T(8,128)(2,1)S(1)}, u32[]{:S(2)}) copy-start(bf16[256,88]{1,0:T(8,128)(2,1)S(1)} %copy.57) | copy-start | bytes 135172
  503.3 140.6 %copy-start.45 = (f32[256]{0:T(256)}, f32[256]{0:T(256)S(1)}, u32[]{:S(2)}) copy-start(f32[256]{0:T(256)S(1)} %broadcast_multiply_fusion.7) | copy-start | bytes 3076
  507.6 10.2 all-to-all-start.3
  511.9 332.1 %all-reduce.12.cloned.1.call-start = ((), (), s32[]{:S(2)}) async-start(), calls=%async_computation.9 | async-start | bytes 1441792 | tf_op jit(solution)/shard_map/psum | solution.py:80
  545.2 77.4 %copy-start.21 = (f32[49,88]{1,0:T(8,128)}, f32[49,88]{1,0:T(8,128)S(1)}, u32[]{:S(2)}) copy-start(f32[49,88]{1,0:T(8,128)S(1)} %psum.119) | copy-start | bytes 51748
  757.5 163.9 %copy-start.7 = (f32[256,1408]{1,0:T(8,128)}, f32[256,1408]{1,0:T(8,128)S(1)}, u32[]{:S(2)}) copy-start(f32[256,1408]{1,0:T(8,128)S(1)} %fusion.8) | copy-start | bytes 4325380
  760.3 160.1 %reduce-scatter.14.cloned.1.call-start = ((), (), s32[]{:S(2)}) async-start(), calls=%async_computation.12 | async-start | bytes 765952
  847.9 126.8 %copy-start.38 = (s32[1024]{0:T(1024)S(1)}, s32[1024]{0:T(1024)}, u32[]{:S(2)}) copy-start(s32[1024]{0:T(1024)} %copy-done.37) | copy-start | bytes 12292
  847.9 128.2 %copy-start.52 = (pred[512]{0:T(512)(128)(4,1)S(1)}, pred[512]{0:T(512)(128)(4,1)}, u32[]{:S(2)}) copy-start(pred[512]{0:T(512)(128)(4,1)} %copy-done.51) | copy-start | bytes 1540
  847.9 128.2 %copy-start.54 = (pred[512]{0:T(512)(128)(4,1)S(1)}, pred[512]{0:T(512)(128)(4,1)}, u32[]{:S(2)}) copy-start(pred[512]{0:T(512)(128)(4,1)} %copy-done.53) | copy-start | bytes 1540
  847.9 154.2 %copy-start.20 = (f32[49,88]{1,0:T(8,128)S(1)}, f32[49,88]{1,0:T(8,128)}, u32[]{:S(2)}) copy-start(f32[49,88]{1,0:T(8,128)} %param.31) | copy-start | bytes 51748
  847.9 154.2 %copy-start.22 = (f32[49,88]{1,0:T(8,128)S(1)}, f32[49,88]{1,0:T(8,128)}, u32[]{:S(2)}) copy-start(f32[49,88]{1,0:T(8,128)} %copy-done.21) | copy-start | bytes 51748
  (37 other events, 274.9 us)
Sparse Core Ops, SparseCore 0:
  224.8 85.8 all-reduce.13
  315.0 72.4 reduce-scatter.11
  390.7 72.2 reduce-scatter.9
  760.4 83.6 all-reduce.11
  848.1 72.2 reduce-scatter.13
where the time goes:
time: 1100 us; the launch traced here: 1090 us
  waiting for transfers between devices  421 us (38%)
  blocking collectives  388 us (35%)
  other arithmetic  169 us (15%)
  local copies, waits for them, and re-layouts  59.9 us (5%)
  starting transfers between devices  17.3 us (2%)
  between operations  17.1 us (2%)
  matrix products  17 us (2%)
    unnamed x8, waiting for transfers between devices  215 us
    psum x5, blocking collectives, inner_model(): return lax.psum(jnp.sum(first_vec * second_vec), 'mp')  191 us
    psum x2, waiting for transfers between devices, model_sum(): lax.psum(partial_value.astype(jnp.bfloat16), 'mp').astype(jnp.float32)  170 us
    convert_element_type x2, other arithmetic, hessian(): depthwise(conv_source, full_direction).astype(jnp.bfloat16)  100 us
    psum x2, blocking collectives, row_stats(): return lax.psum((first_sum, second_sum), 'mp')  76.1 us
    psum x2, blocking collectives, hessian(): return (lax.psum(local_term, 'dp'), local_term)  47.7 us
    all_gather x2, blocking collectives, hessian(): full_direction = lax.all_gather(direction, 'mp', axis=1, tiled=True)  42.2 us
    all_to_all x1, waiting for transfers between devices, per_device(): lax.all_to_all(pack_slots(payload), 'dp', split_axis=0, concat_axis=0, ti...  24.6 us
  transfers between devices with their start and end apart: 9, of which 8 were waited for; matrix products, arithmetic and copies ran while one was open for 9% of the time, Pallas kernels for 0%

commit v1 on v0

--- a/solution.py
+++ b/solution.py
@@ -12,6 +12,9 @@
 vector_eps = 1e-06
 half_root = 0.7071067811865476
 density_scale = 0.3989422804014327
+record_mix = lambda local: jnp.concatenate(
+    lax.all_to_all(jnp.stack(lax.axis_size("mp") * [local], axis=0), "mp", 0, 0), axis=1
+)
 
 
 def phi_density(values):
@@ -187,7 +190,7 @@
     safe_slots = jnp.maximum(flat_slots, 0)
 
     def hessian(direction):
-        full_direction = lax.all_gather(direction, "mp", axis=1, tiled=True)
+        full_direction = record_mix(direction)
         tangent = depthwise(conv_source, full_direction).astype(jnp.bfloat16).reshape(cell_count, C)
         arrived_tan = lax.all_to_all(
             pack_slots(tangent), "dp", split_axis=0, concat_axis=0, tiled=True

time: 1100 us -> 1170 us (1.064)
  other arithmetic: 169 us -> 228 us
  local copies, waits for them, and re-layouts: 59.9 us -> 97.7 us
  blocking collectives: 388 us -> 358 us
    convert_element_type x2, other arithmetic: 100 us -> 161 us  [hessian(): depthwise(conv_source, full_direction).astype(jnp.bfloat16)]
    all_gather x2 -> x0, blocking collectives: 42.2 us -> none  [hessian(): full_direction = lax.all_gather(direction, 'mp', axis=1, tiled=True)]
    mul x0 -> x98, local copies, waits for them, and re-layouts: none -> 37.1 us  [depthwise(): padded[:, tap_row:tap_row + SIDE, tap_col:tap_col + SIDE, :]]
    all_to_all x0 -> x1, blocking collectives: none -> 12.4 us  [lax.all_to_all(jnp.stack(lax.axis_size('mp') * [local], axis=0), 'mp', 0, 0)]
  transfers between devices with their start and end apart: 9 -> 10, of which waited for: 8 -> 8; matrix products, arithmetic and copies ran while one was open for 9% -> 14% of each run, Pallas kernels for 0% -> 0%
where the time goes in v1:
time: 1170 us; the launch traced here: 1160 us
  waiting for transfers between devices  420 us (36%)
  blocking collectives  358 us (31%)
  other arithmetic  228 us (19%)
  local copies, waits for them, and re-layouts  97.7 us (8%)
  starting transfers between devices  21.3 us (2%)
  between operations  17.5 us (1%)
  matrix products  17 us (1%)
    unnamed x8, waiting for transfers between devices  215 us
    psum x5, blocking collectives, inner_model(): return lax.psum(jnp.sum(first_vec * second_vec), 'mp')  191 us
    psum x2, waiting for transfers between devices, model_sum(): lax.psum(partial_value.astype(jnp.bfloat16), 'mp').astype(jnp.float32)  169 us
    convert_element_type x2, other arithmetic, hessian(): depthwise(conv_source, full_direction).astype(jnp.bfloat16)  161 us
    psum x2, blocking collectives, row_stats(): return lax.psum((first_sum, second_sum), 'mp')  76.1 us
    psum x2, blocking collectives, hessian(): return (lax.psum(local_term, 'dp'), local_term)  47.7 us
    mul x98, local copies, waits for them, and re-layouts, depthwise(): padded[:, tap_row:tap_row + SIDE, tap_col:tap_col + SIDE, :]  37.1 us
    all_to_all x1, waiting for transfers between devices, per_device(): lax.all_to_all(pack_slots(payload), 'dp', split_axis=0, concat_axis=0, ti...  24.8 us
  transfers between devices with their start and end apart: 10, of which 8 were waited for; matrix products, arithmetic and copies ran while one was open for 14% of the time, Pallas kernels for 0%

profile of v1, /device:TPU:0, one launch (start us, length us, event | category | flops | bytes accessed | tf_op | source)
XLA Modules:
  0.0 1160.1 jit_solution(12982487784986634606)
XLA Ops:
  8.7 42.7 %psum.112 = f32[]{:T(128)} all-reduce(f32[]{:T(128)} %multiply_reduce_fusion.5), channel_id=1, replica_groups=mesh['dp'=8,'mp'=16] {'mp'}, use_global_device_ids=true, to_apply=%region_8.9 | all-reduce | flops 1 | bytes 8 | tf_op jit(solution)/shard_map/psum | solution.py:97
  65.3 19.7 %add_convert_fusion.2 = bf16[2,16,16,1408]{3,2,1,0:T(8,128)(2,1)S(1)} fusion(bf16[2,16,16,1408]{3,2,1,0:T(8,128)(2,1)S(1)} %get-tuple-element.279, f32[2,16,16,1408]{3,2,1,0:T(8,128)S(1)} %get-tuple-element.278, f32[1408]{0:T(1024)S(1)} %copy-done.48, f32[1408]{0:T(1024)S(1)} %get-tuple-element.158, f32[1408]{0:T(1024)S(1)} %get-tuple-element.159, ...), kind=kLoop, calls=%fused_computation.160 | loop fusion | flops 72089600 | bytes 6048768 | tf_op jit(solution)/shard_map/convert_element_type | solution.py:143
  89.8 8.1 pad_maximum_fusion
  98.0 4.1 copy.738
  102.7 4.3 all-to-all-start
  112.5 80.7 %add_convert_fusion.1 = bf16[2,16,16,1408]{3,2,1,0:T(8,128)(2,1)S(1)} fusion(bf16[2,16,16,1408]{3,2,1,0:T(8,128)(2,1)} %copy-done.3, f32[2,16,16,1408]{3,2,1,0:T(8,128)} %copy-done.1, f32[1408]{0:T(1024)S(1)} %mul.2012, f32[1408]{0:T(1024)S(1)} %mul.2009, f32[1408]{0:T(1024)S(1)} %mul.2006, f32[1408]{0:T(1024)S(1)} %mul.2003, f32[1408]{0:T(1024)S(1)} %mul.2000, ...), kind=kLoop, calls=%fused_computation.158 | loop fusion | flops 71368704 | bytes 6043136 | tf_op jit(solution)/shard_map/convert_element_type | solution.py:194
  198.6 4.8 all-to-all-start.3
  203.4 8.7 gather_fusion
  215.6 6.1 all-to-all-done.3
  228.9 4.2 gather_fusion.3
  233.1 24.8 %all-to-all-done.1 = bf16[8,56,2816]{2,1,0:T(8,128)(2,1)S(1)} async-done(((bf16[8,56,2816]{2,1,0:T(8,128)(2,1)}), bf16[8,56,2816]{2,1,0:T(8,128)(2,1)S(1)}, u32[]{:S(2)}, u32[]{:S(2)}) %all-to-all-start.1) | async-done | bytes 2523168 | tf_op jit(solution)/shard_map/all_to_all | solution.py:149
  273.2 87.7 %all-reduce.14.cloned.1.call-done = (bf16[256,1408]{1,0:T(8,128)(2,1)}, bf16[256,1408]{1,0:T(8,128)(2,1)}) async-done(((bf16[256,1408]{1,0:T(8,128)(2,1)}, bf16[256,1408]{1,0:T(8,128)(2,1)}), (bf16[256,1408]{1,0:T(8,128)(2,1)}, bf16[256,1408]{1,0:T(8,128)(2,1)})) %all-reduce.14.cloned.1.call-update) | async-done | bytes 1441808 | tf_op jit(solution)/shard_map/psum | solution.py:83
  365.1 3.7 convolution_convert_fusion.3
  370.1 67.5 %reduce-scatter.12.cloned.1.call-done = bf16[256,88]{0,1:T(8,128)(2,1)} async-done(((bf16[256,1408]{0,1:T(8,128)(2,1)}), bf16[256,88]{0,1:T(8,128)(2,1)}) %reduce-scatter.12.cloned.1.call-update) | async-done | bytes 45072
  438.5 74.6 %reduce-scatter.10.cloned.1.call-done = bf16[256,88]{0,1:T(8,128)(2,1)} async-done(((bf16[256,1408]{0,1:T(8,128)(2,1)}), bf16[256,88]{0,1:T(8,128)(2,1)}) %reduce-scatter.10.cloned.1.call-update) | async-done | bytes 45072
  515.4 38.1 %all-reduce.7 = (f32[256]{0:T(256)S(1)}, f32[256]{0:T(256)S(1)}, f32[256]{0:T(256)S(1)}, f32[256]{0:T(256)S(1)}) all-reduce(f32[256]{0:T(256)S(1)} %get-tuple-element.261, f32[256]{0:T(256)S(1)} %get-tuple-element.8, f32[256]{0:T(256)S(1)} %get-tuple-element.6, f32[256]{0:T(256)S(1)} %get-tuple-element.258), channel_id=1, replica_groups=mesh['dp'=8,'mp'=16] {'mp'}, use_global_device_ids=true, to_apply=%region_22.25 | all-reduce | flops 1024 | bytes 8192 | tf_op jit(solution)/shard_map/psum | solution.py:93
  557.8 4.3 all-to-all-start.4
  562.3 5.7 all-to-all-done.4
  571.5 23.9 %psum.119 = f32[49,88]{1,0:T(8,128)S(1)} all-reduce(f32[49,88]{1,0:T(8,128)S(1)} %broadcast_multiply_fusion.2), channel_id=1, replica_groups=mesh['dp'=8,'mp'=16] {'dp'}, use_global_device_ids=true, to_apply=%region_23.28 | all-reduce | flops 4312 | bytes 34496 | tf_op jit(solution)/shard_map/psum | solution.py:244
  596.0 36.1 %psum.120 = f32[]{:T(128)} all-reduce(f32[]{:T(128)} %multiply_reduce_fusion.4), channel_id=1, replica_groups=mesh['dp'=8,'mp'=16] {'mp'}, use_global_device_ids=true, to_apply=%region_25.30 | all-reduce | flops 1 | bytes 8 | tf_op jit(solution)/shard_map/psum | solution.py:97
  633.3 38.1 %psum.121 = f32[]{:T(128)} all-reduce(f32[]{:T(128)} %multiply_reduce_fusion.3), channel_id=1, replica_groups=mesh['dp'=8,'mp'=16] {'mp'}, use_global_device_ids=true, to_apply=%region_27.32 | all-reduce | flops 1 | bytes 8 | tf_op jit(solution)/shard_map/psum | solution.py:97
  672.9 12.4 %all_to_all.41 = f32[16,49,88]{2,1,0:T(8,128)S(1)} all-to-all(f32[16,49,88]{2,1,0:T(8,128)S(1)} %stack.408), channel_id=1, replica_groups=mesh['dp'=8,'mp'=16] {'mp'}, dimensions={0} | all-to-all | bytes 551936 | tf_op jit(solution)/shard_map/all_to_all | solution.py:16
  719.7 80.6 %add_convert_fusion = bf16[2,16,16,1408]{3,2,1,0:T(8,128)(2,1)S(1)} fusion(bf16[2,16,16,1408]{3,2,1,0:T(8,128)(2,1)} %copy-done.3, f32[2,16,16,1408]{3,2,1,0:T(8,128)} %copy-done.1, f32[1408]{0:T(1024)} %mul.2190, f32[1408]{0:T(1024)} %mul.2187, f32[1408]{0:T(1024)} %mul.2184, f32[1408]{0:T(1024)} %mul.2181, f32[1408]{0:T(1024)} %mul.2178, f32[1408]{0:T(1024)} %mul.2175, ...), kind=kLoop, calls=%fused_computation.157 | loop fusion | flops 71368704 | bytes 6043136 | tf_op jit(solution)/shard_map/convert_element_type | solution.py:194
  804.8 20.9 %all_to_all.42 = bf16[8,56,1408]{2,1,0:T(8,128)(2,1)S(1)} all-to-all(bf16[8,56,1408]{2,1,0:T(8,128)(2,1)S(1)} %bitcast.820), channel_id=1, replica_groups=mesh['dp'=8,'mp'=16] {'dp'}, dimensions={0} | all-to-all | bytes 2523136 | tf_op jit(solution)/shard_map/all_to_all | solution.py:195
  835.3 81.4 %all-reduce.12.cloned.1.call-done = bf16[256,1408]{1,0:T(8,128)(2,1)} async-done(((bf16[256,1408]{1,0:T(8,128)(2,1)}), bf16[256,1408]{1,0:T(8,128)(2,1)}) %all-reduce.12.cloned.1.call-update) | async-done | bytes 720912 | tf_op jit(solution)/shard_map/psum | solution.py:83
  916.7 3.9 convolution_convert_fusion
  920.6 72.4 %reduce-scatter.14.cloned.1.call-done = bf16[256,88]{0,1:T(8,128)(2,1)} async-done(((bf16[256,1408]{0,1:T(8,128)(2,1)}), bf16[256,88]{0,1:T(8,128)(2,1)}) %reduce-scatter.14.cloned.1.call-update) | async-done | bytes 45072
  995.2 38.1 %all-reduce.6 = (f32[256]{0:T(256)S(1)}, f32[256]{0:T(256)S(1)}) all-reduce(f32[256]{0:T(256)S(1)} %get-tuple-element.260, f32[256]{0:T(256)S(1)} %get-tuple-element.259), channel_id=1, replica_groups=mesh['dp'=8,'mp'=16] {'mp'}, use_global_device_ids=true, to_apply=%region_35.40 | all-reduce | flops 512 | bytes 4096 | tf_op jit(solution)/shard_map/psum | solution.py:93
  1037.2 10.0 all_to_all.43
  1050.8 23.9 %psum.125 = f32[49,88]{1,0:T(8,128)S(1)} all-reduce(f32[49,88]{1,0:T(8,128)S(1)} %broadcast_multiply_fusion.1), channel_id=1, replica_groups=mesh['dp'=8,'mp'=16] {'dp'}, use_global_device_ids=true, to_apply=%region_36.41 | all-reduce | flops 4312 | bytes 34496 | tf_op jit(solution)/shard_map/psum | solution.py:244
  1075.3 36.2 %psum.126 = f32[]{:T(128)} all-reduce(f32[]{:T(128)} %multiply_reduce_fusion.2), channel_id=1, replica_groups=mesh['dp'=8,'mp'=16] {'mp'}, use_global_device_ids=true, to_apply=%region_38.43 | all-reduce | flops 1 | bytes 8 | tf_op jit(solution)/shard_map/psum | solution.py:97
  1112.7 38.1 %psum.127 = f32[]{:T(128)} all-reduce(f32[]{:T(128)} %get-tuple-element.272), channel_id=1, replica_groups=mesh['dp'=8,'mp'=16] {'mp'}, use_global_device_ids=true, to_apply=%region_40.45 | all-reduce | flops 1 | bytes 8 | tf_op jit(solution)/shard_map/psum | solution.py:97
  (353 shorter events, 137.2 us)
Async XLA Ops:
  7.2 262.9 %copy-start = (bf16[352,1408]{1,0:T(8,128)(2,1)S(1)}, bf16[352,1408]{1,0:T(8,128)(2,1)}, u32[]{:S(2)}) copy-start(bf16[352,1408]{1,0:T(8,128)(2,1)} %param.29) | copy-start | bytes 2973700
  53.6 49.1 %all-to-all-start.2 = ((f32[16,49,88]{2,1,0:T(8,128)}), f32[16,49,88]{2,1,0:T(8,128)S(1)}, u32[]{:S(2)}, u32[]{:S(2)}) async-start(f32[16,49,88]{2,1,0:T(8,128)} %stack.357), calls=%async_computation.2 | async-start | bytes 917504 | tf_op jit(solution)/shard_map/all_to_all | solution.py:16
  63.4 132.6 %copy-start.55 = (pred[448]{0:T(512)(128)(4,1)}, pred[448]{0:T(512)(128)(4,1)S(1)}, u32[]{:S(2)}) copy-start(pred[448]{0:T(512)(128)(4,1)S(1)} %compare_and_fusion.2) | copy-start | bytes 1348
  97.9 95.3 %copy-start.35 = (s32[1024]{0:T(1024)}, s32[1024]{0:T(1024)S(1)}, u32[]{:S(2)}) copy-start(s32[1024]{0:T(1024)S(1)} %pad_clamp_fusion.3) | copy-start | bytes 12292
  102.7 95.8 %all-to-all-start = ((bf16[8,1,56]{2,1,0:T(2,128)(2,1)}), bf16[8,1,56]{2,1,0:T(2,128)(2,1)S(1)}, u32[]{:S(2)}, u32[]{:S(2)}) async-start(bf16[8,1,56]{2,1,0:T(2,128)(2,1)} %reshape.1062), calls=%async_computation | async-start | bytes 8192 | tf_op jit(solution)/shard_map/all_to_all | solution.py:150
  198.6 23.0 %all-to-all-start.3 = ((bf16[8,56,1408]{2,1,0:T(8,128)(2,1)}), bf16[8,56,1408]{2,1,0:T(8,128)(2,1)S(1)}, u32[]{:S(2)}, u32[]{:S(2)}) async-start(bf16[8,56,1408]{2,1,0:T(8,128)(2,1)} %bitcast.210), calls=%async_computation.3 | async-start | bytes 2523136 | tf_op jit(solution)/shard_map/all_to_all | solution.py:195
  222.7 35.3 %all-to-all-start.1 = ((bf16[8,56,2816]{2,1,0:T(8,128)(2,1)}), bf16[8,56,2816]{2,1,0:T(8,128)(2,1)S(1)}, u32[]{:S(2)}, u32[]{:S(2)}) async-start(bf16[8,56,2816]{2,1,0:T(8,128)(2,1)} %broadcast_select_fusion), calls=%async_computation.1 | async-start | bytes 5046272 | tf_op jit(solution)/shard_map/all_to_all | solution.py:149
  226.3 134.6 %all-reduce.14.cloned.1.call-start = ((), (), s32[]{:S(2)}) async-start(), calls=%async_computation.15 | async-start | bytes 2883584 | tf_op jit(solution)/shard_map/psum | solution.py:83
  265.5 95.4 %copy-start.4 = (bf16[256,2,1408]{2,0,1:T(8,128)(2,1)}, bf16[256,2,1408]{2,0,1:T(8,128)(2,1)S(1)}, u32[]{:S(2)}) copy-start(bf16[256,2,1408]{2,0,1:T(8,128)(2,1)S(1)} %broadcast_select_fusion.1) | copy-start | bytes 4325380
  273.1 164.5 %reduce-scatter.12.cloned.1.call-start = ((), (), s32[]{:S(2)}) async-start(), calls=%async_computation.13 | async-start | bytes 765952
  365.0 148.1 %reduce-scatter.10.cloned.1.call-start = ((), (), s32[]{:S(2)}) async-start(), calls=%async_computation.12 | async-start | bytes 765952
  365.1 189.0 %copy-start.27 = (f32[256]{0:T(256)S(1)}, f32[256]{0:T(256)}, u32[]{:S(2)}) copy-start(f32[256]{0:T(256)} %copy-done.26) | copy-start | bytes 3076
  365.1 189.0 %copy-start.56 = (f32[256]{0:T(256)S(1)}, f32[256]{0:T(256)}, u32[]{:S(2)}) copy-start(f32[256]{0:T(256)} %get-tuple-element.285) | copy-start | bytes 3076
  365.1 191.9 %copy-start.44 = (pred[448]{0:T(512)(128)(4,1)S(1)}, pred[448]{0:T(512)(128)(4,1)}, u32[]{:S(2)}) copy-start(pred[448]{0:T(512)(128)(4,1)} %copy-done.43) | copy-start | bytes 1348
  365.1 191.9 %copy-start.50 = (pred[448]{0:T(512)(128)(4,1)S(1)}, pred[448]{0:T(512)(128)(4,1)}, u32[]{:S(2)}) copy-start(pred[448]{0:T(512)(128)(4,1)} %get-tuple-element.276) | copy-start | bytes 1348
  368.8 226.6 %copy-start.19 = (f32[49,88]{1,0:T(8,128)S(1)}, f32[49,88]{1,0:T(8,128)}, u32[]{:S(2)}) copy-start(f32[49,88]{1,0:T(8,128)} %param.31) | copy-start | bytes 51748
  368.9 184.6 %copy-start.49 = (f32[88]{0:T(128)}, f32[88]{0:T(128)S(1)}, u32[]{:S(2)}) copy-start(f32[88]{0:T(128)S(1)} %dynamic_slice.16) | copy-start | bytes 1060
  370.0 302.9 %copy-start.51 = (pred[512]{0:T(512)(128)(4,1)}, pred[512]{0:T(512)(128)(4,1)S(1)}, u32[]{:S(2)}) copy-start(pred[512]{0:T(512)(128)(4,1)S(1)} %get-tuple-element.281) | copy-start | bytes 1540
  370.0 302.9 %copy-start.53 = (pred[512]{0:T(512)(128)(4,1)}, pred[512]{0:T(512)(128)(4,1)S(1)}, u32[]{:S(2)}) copy-start(pred[512]{0:T(512)(128)(4,1)S(1)} %get-tuple-element.282) | copy-start | bytes 1540
  370.1 198.0 %copy-start.36 = (s32[1024]{0:T(1024)}, s32[1024]{0:T(1024)S(1)}, u32[]{:S(2)}) copy-start(s32[1024]{0:T(1024)S(1)} %pad_clamp_fusion.1) | copy-start | bytes 12292
  438.5 119.3 %copy-start.14 = (bf16[256,88]{1,0:T(8,128)(2,1)}, bf16[256,88]{1,0:T(8,128)(2,1)S(1)}, u32[]{:S(2)}) copy-start(bf16[256,88]{1,0:T(8,128)(2,1)S(1)} %copy.50) | copy-start | bytes 135172
  553.5 131.8 %copy-start.45 = (f32[256]{0:T(256)}, f32[256]{0:T(256)S(1)}, u32[]{:S(2)}) copy-start(f32[256]{0:T(256)S(1)} %broadcast_multiply_fusion.7) | copy-start | bytes 3076
  557.8 10.2 all-to-all-start.4
  562.1 354.6 %all-reduce.12.cloned.1.call-start = ((), (), s32[]{:S(2)}) async-start(), calls=%async_computation.11 | async-start | bytes 1441792 | tf_op jit(solution)/shard_map/psum | solution.py:83
  562.3 122.9 %copy-start.37 = (s32[1024]{0:T(1024)}, s32[1024]{0:T(1024)S(1)}, u32[]{:S(2)}) copy-start(s32[1024]{0:T(1024)S(1)} %pad_clamp_fusion) | copy-start | bytes 12292
  832.4 161.6 %copy-start.7 = (f32[256,1408]{1,0:T(8,128)}, f32[256,1408]{1,0:T(8,128)S(1)}, u32[]{:S(2)}) copy-start(f32[256,1408]{1,0:T(8,128)S(1)} %fusion.8) | copy-start | bytes 4325380
  835.2 157.9 %reduce-scatter.14.cloned.1.call-start = ((), (), s32[]{:S(2)}) async-start(), calls=%async_computation.14 | async-start | bytes 765952
  920.6 126.6 %copy-start.38 = (s32[1024]{0:T(1024)S(1)}, s32[1024]{0:T(1024)}, u32[]{:S(2)}) copy-start(s32[1024]{0:T(1024)} %copy-done.37) | copy-start | bytes 12292
  920.6 128.0 %copy-start.52 = (pred[512]{0:T(512)(128)(4,1)S(1)}, pred[512]{0:T(512)(128)(4,1)}, u32[]{:S(2)}) copy-start(pred[512]{0:T(512)(128)(4,1)} %copy-done.51) | copy-start | bytes 1540
  920.6 128.0 %copy-start.54 = (pred[512]{0:T(512)(128)(4,1)S(1)}, pred[512]{0:T(512)(128)(4,1)}, u32[]{:S(2)}) copy-start(pred[512]{0:T(512)(128)(4,1)} %copy-done.53) | copy-start | bytes 1540
  920.6 154.0 %copy-start.22 = (f32[49,88]{1,0:T(8,128)S(1)}, f32[49,88]{1,0:T(8,128)}, u32[]{:S(2)}) copy-start(f32[49,88]{1,0:T(8,128)} %copy-done.21) | copy-start | bytes 51748
  920.6 190.8 %copy-start.20 = (f32[49,88]{1,0:T(8,128)S(1)}, f32[49,88]{1,0:T(8,128)}, u32[]{:S(2)}) copy-start(f32[49,88]{1,0:T(8,128)} %param.31) | copy-start | bytes 51748
  (38 other events, 353.6 us)
Sparse Core Ops, SparseCore 0:
  273.2 87.6 all-reduce.13
  365.1 72.4 reduce-scatter.11
  440.9 72.2 reduce-scatter.9
  835.4 81.3 all-reduce.11
  920.8 72.2 reduce-scatter.13
